TPU v7x, 32 devices: a whole 2x2x4 slice. The times are simulated.
32 devices in a mesh: dp: 4 (over y, x), section: 2 (over core), tensor: 4 (over z).
Axes of the slice: x: 2, y: 2, z: 4, core: 2. Of those that a mesh axis runs over, the one named last changes fastest.
Arguments:
- in_delta: bfloat16 [8, 1024, 4096], P(None, ('dp', 'tensor')), may hold values from -12 to 12
- weight: bfloat16 [2, 4096, 4096], P('section', 'tensor'), may hold values from -0.09375 to 0.09375
- cache_codes: int32 [2, 2, 8, 1024, 4096], P('section', None, None, ('dp', 'tensor')), may hold values from -7 to 7, as said below
- cache_scales: float32 [2, 2, 8, 4, 32], P('section', None, None, 'dp'), may hold values from 0.2 to 6, as said below
- cotangent: bfloat16 [8, 1024, 4096], P(None, ('dp', 'tensor')), may hold values from -6 to 6
Outputs:
- out_deltas: bfloat16 [2, 8, 1024, 4096], P('section', None, ('dp', 'tensor'))
- grad_in: bfloat16 [2, 8, 1024, 4096], P('section', None, ('dp', 'tensor'))
- weight_grad: float32 [2, 4096, 4096], P('section', 'tensor', 'dp')
Inputs may be any that keep to these rules, and one draw needn't show every extreme that they name: cache_codes[s, 1] equals cache_codes[s + 1, 0]: the buffer of a boundary between two segments is held by both. cache_scales[s, 1] equals cache_scales[s + 1, 0].
All inputs are finite; a program needn't handle non-finite values. Where the computation divides by a largest or mean magnitude, that divisor is 1e-20 or more.
Results may differ from a plain program's by a relative error of at most 0.013.
Values may be sent and summed in bfloat16 or wider, within the bound.
A program may use at most 320 MiB of HBM per device.

v0:
```python
import jax
import jax.numpy as jnp
from jax import lax
from jax.sharding import PartitionSpec as P

code_levels = 7.0
softness = 0.8
two_pi = 6.283185307179586
epsilon = 1e-06
bf16 = jnp.bfloat16
f32 = jnp.float32
chunk_count = 1
sine_terms = (
    6.283185307179586,
    -41.34170224039975,
    81.60524927607504,
    -76.70585975306136,
    42.058693944897655,
    -15.094642576822984,
    3.819952584848282,
)


def sine_of_turns(turns):
    rest = turns - jnp.round(turns)
    rest = jnp.where(rest > 0.25, 0.5 - rest, jnp.where(rest < -0.25, -0.5 - rest, rest))
    square = rest * rest
    total = jnp.full_like(rest, sine_terms[-1])
    for term in sine_terms[-2::-1]:
        total = total * square + term
    return total * rest


def local(in_delta, weight, cache_codes, cache_scales, cotangent):
    dp_count = lax.axis_size("dp")
    section_count = lax.axis_size("section")
    replica = lax.axis_index("dp")
    first = lax.axis_index("section") == 0
    micro_count, rows, width = in_delta.shape
    block_count = cache_scales.shape[-1]
    block = width // block_count
    part = width // dp_count
    is_power = dp_count & dp_count - 1 == 0
    chunks = chunk_count if micro_count % chunk_count == 0 else 1
    micros = micro_count // chunks
    tokens = micros * rows

    def target(source, step):
        return source ^ step if is_power else (source + step) % dp_count

    def origin(source, step):
        return source ^ step if is_power else (source - step) % dp_count

    def exchange(value, section, step):
        pairs = [
            (source * section_count + section, target(source, step) * section_count + section)
            for source in range(dp_count)
        ]
        return lax.ppermute(value, ("dp", "section"), pairs)

    def give_back(value, section, step):
        pairs = [
            (source * section_count + section, origin(source, step) * section_count + section)
            for source in range(dp_count)
        ]
        return lax.ppermute(value, ("dp", "section"), pairs)

    def columns(value, index):
        return lax.dynamic_slice_in_dim(value, index * part, part, 1)

    weight_part = lax.all_gather(columns(weight[0], replica), "tensor", axis=0, tiled=True)

    def product(forward_here, whole, piece):

        def forward(whole, piece):
            out = jnp.dot(whole, weight_part, preferred_element_type=f32).astype(bf16)
            return (out, jnp.zeros((tokens, width), bf16))

        def backward(whole, piece):
            out = lax.dot_general(
                piece, weight_part, (((1,), (1,)), ((), ())), preferred_element_type=f32
            ).astype(bf16)
            return (jnp.zeros((tokens, part), bf16), out)

        return lax.cond(forward_here, forward, backward, whole, piece)

    def pre(normed, upstream, forward_section):
        whole, piece = ([normed], [columns(upstream, replica)])
        for step in range(1, dp_count):
            whole.append(exchange(normed, forward_section, step))
            piece.append(
                exchange(columns(upstream, target(replica, step)), 1 - forward_section, step)
            )
        return (whole, piece)

    def middle(whole, piece, forward_section):
        here = first if forward_section == 0 else ~first
        branch = jnp.zeros((tokens, width), bf16)
        grad = None
        order = list(range(1, dp_count)) + [0]
        for step in order:
            out, back = product(here, whole[step], piece[step])
            if step:
                out = give_back(out, forward_section, step)
                back = give_back(back, 1 - forward_section, step)
            branch = lax.dynamic_update_slice_in_dim(branch, out, target(replica, step) * part, 1)
            grad = back.astype(f32) if grad is None else grad + back.astype(f32)
        return (branch, grad)

    def scales_row(slot, chunk):
        now = cache_scales[0, slot, chunk * micros : (chunk + 1) * micros, 0]
        return jnp.repeat(now / code_levels, block, axis=-1)[:, None, :]

    def codes(slot, chunk):
        return cache_codes[0, slot, chunk * micros : (chunk + 1) * micros].astype(f32)

    def shaped(value):
        return value.reshape(micros, rows, width)

    def flat(value):
        return value.reshape(tokens, width)

    def rms(hidden):
        return lax.rsqrt(jnp.mean(hidden * hidden, axis=-1, keepdims=True) + epsilon)

    def finish_forward(hidden, branch, chunk):
        delta = hidden + shaped(branch).astype(f32) - codes(1, chunk) * scales_row(1, chunk)
        peak = jnp.max(jnp.abs(delta), axis=1).reshape(micros, block_count, block).max(axis=-1)
        spread = lax.pmax(peak, "tensor") + epsilon
        up_scale = jnp.repeat(code_levels / spread, block, axis=-1)[:, None, :]
        down_scale = jnp.repeat(spread / code_levels, block, axis=-1)[:, None, :]
        level = delta * up_scale
        smooth = level - softness / two_pi * sine_of_turns(level)
        return (smooth * down_scale).astype(bf16)

    def finish_backward(hidden, upstream, grad):
        inverse = rms(hidden)
        grad = shaped(grad.astype(bf16)).astype(f32)
        unrounded = hidden * inverse
        mean = jnp.mean(grad * unrounded, axis=-1, keepdims=True)
        return (upstream.astype(f32) + inverse * (grad - unrounded * mean)).astype(bf16)

    over = range(chunks)
    span = [slice(c * micros, (c + 1) * micros) for c in over]
    outs, grads, wholes, pieces = ([None] * chunks, [None] * chunks, [], [])
    with jax.named_scope("phase_a"):
        stage_a = []
        for c in over:
            hidden = codes(0, c) * scales_row(0, c) + in_delta[span[c]].astype(f32)
            normed = flat((hidden * rms(hidden)).astype(bf16))
            stage_a.append((hidden, pre(normed, flat(cotangent[span[c]]), 0)))
        stage_b = []
        for c in over:
            hidden, (whole, piece) = stage_a[c]
            branch, grad = middle(whole, piece, 0)
            outs[c] = finish_forward(hidden, branch, c)
            received = lax.ppermute(outs[c], "section", [(0, 1)])
            incoming = jnp.where(first, in_delta[span[c]], received)
            hidden = codes(0, c) * scales_row(0, c) + incoming.astype(f32)
            normed = flat((hidden * rms(hidden)).astype(bf16))
            grads[c] = finish_backward(hidden, cotangent[span[c]], grad)
            upstream = lax.ppermute(grads[c], "section", [(1, 0)])
            stage_b.append((hidden, upstream, pre(normed, flat(upstream), 1)))
    with jax.named_scope("weight_grad"):

        def gathered(pairs):
            whole = jnp.concatenate([w for p in pairs for w in p[0]], axis=0)
            piece = jnp.concatenate([g for p in pairs for g in p[1]], axis=0)
            return lax.dot_general(
                whole, piece, (((0,), (0,)), ((), ())), preferred_element_type=f32
            ).astype(bf16)

        from_a = [a[1] for a in stage_a]
        from_b = [b[2] for b in stage_b]
        partial = lax.cond(
            first,
            lambda a, b: gathered([(x[0], y[1]) for x, y in zip(a, b)]),
            lambda a, b: gathered([(y[0], x[1]) for x, y in zip(a, b)]),
            from_a,
            from_b,
        )
        weight_grad = lax.psum_scatter(partial, "tensor", scatter_dimension=0, tiled=True).astype(
            f32
        )
    with jax.named_scope("phase_b"):
        for c in over:
            hidden, upstream, (whole, piece) = stage_b[c]
            branch, grad = middle(whole, piece, 1)
            outs[c] = jnp.where(first, outs[c], finish_forward(hidden, branch, c))
            grads[c] = jnp.where(first, finish_backward(hidden, upstream, grad), grads[c])

    def joined(values):
        return values[0] if chunks == 1 else jnp.concatenate(values, axis=0)

    return (joined(outs)[None], joined(grads)[None], weight_grad[None])


def solution(mesh):
    return jax.shard_map(
        local,
        mesh=mesh,
        in_specs=(
            P(None, ("dp", "tensor"), None),
            P("section", "tensor", None),
            P("section", None, None, ("dp", "tensor"), None),
            P("section", None, None, "dp", None),
            P(None, ("dp", "tensor"), None),
        ),
        out_specs=(
            P("section", None, ("dp", "tensor"), None),
            P("section", None, ("dp", "tensor"), None),
            P("section", "tensor", "dp"),
        ),
        check_vma=False,
    )
```

profile of v0, /device:TPU:0, one launch (start us, length us, event | category | flops | bytes accessed | tf_op | source)
XLA Modules:
  0.0 650.8 jit_solution(17518955438547281373)
XLA Ops:
  42.7 120.1 %all-gather.3.cloned.1.call-done = bf16[1,4096,1024]{2,1,0:T(8,128)(2,1)} async-done(((bf16[1,1024,1024]{2,1,0:T(8,128)(2,1)}), bf16[1,4096,1024]{2,1,0:T(8,128)(2,1)}) %all-gather.3.cloned.1.call-update) | async-done | bytes 8388624 | tf_op jit(solution)/shard_map/all_gather | solution.py:71
  162.8 10.8 %conditional.13 = (bf16[512,1024]{1,0:T(8,128)(2,1)}, bf16[512,4096]{1,0:T(8,128)(2,1)S(1)}) conditional(s32[]{:T(128)} %convert_element_type.174, (bf16[512,1024]{1,0:T(8,128)(2,1)}, bf16[4096,1024]{1,0:T(8,128)(2,1)}) %tuple.157, (bf16[512,4096]{1,0:T(8,128)(2,1)}, bf16[4096,1024]{1,0:T(8,128)(2,1)}) %tuple.142), branch_computations={%region_1.0_spmd, %region_2.0_spmd} | conditional | flops 4297064448 | bytes 17825810 | solution.py:85
  162.8 10.3 %convolution_convert_fusion.1 = bf16[512,1024]{1,0:T(8,128)(2,1)} fusion(bf16[512,4096]{1,0:T(8,128)(2,1)} %get-tuple-element.105, bf16[4096,1024]{1,0:T(8,128)(2,1)} %get-tuple-element.106), kind=kOutput, calls=%fused_computation.1 | convolution fusion | flops 4295491584 | bytes 13631488 | tf_op jit(solution)/shard_map/phase_a/cond/branch_1_fun/dot_general | solution.py:76
  177.1 10.9 %conditional.14 = (bf16[512,1024]{1,0:T(8,128)(2,1)}, bf16[512,4096]{1,0:T(8,128)(2,1)S(1)}) conditional(s32[]{:T(128)} %convert_element_type.174, (bf16[512,1024]{1,0:T(8,128)(2,1)}, bf16[4096,1024]{1,0:T(8,128)(2,1)}) %tuple.143, (bf16[512,4096]{1,0:T(8,128)(2,1)}, bf16[4096,1024]{1,0:T(8,128)(2,1)}) %tuple.144), branch_computations={%region_3.0_spmd, %region_4.0_spmd} | conditional | flops 4297064448 | bytes 17825810 | solution.py:85
  177.3 10.1 %convolution_convert_fusion.3 = bf16[512,1024]{1,0:T(8,128)(2,1)} fusion(bf16[512,4096]{1,0:T(8,128)(2,1)} %get-tuple-element.109, bf16[4096,1024]{1,0:T(8,128)(2,1)} %get-tuple-element.110), kind=kOutput, calls=%fused_computation.3 | convolution fusion | flops 4295491584 | bytes 13631488 | tf_op jit(solution)/shard_map/phase_a/cond/branch_1_fun/dot_general | solution.py:76
  191.4 11.1 %conditional.15 = (bf16[512,1024]{1,0:T(8,128)(2,1)}, bf16[512,4096]{1,0:T(8,128)(2,1)S(1)}) conditional(s32[]{:T(128)} %convert_element_type.174, (bf16[512,1024]{1,0:T(8,128)(2,1)}, bf16[4096,1024]{1,0:T(8,128)(2,1)}) %tuple.145, (bf16[512,4096]{1,0:T(8,128)(2,1)}, bf16[4096,1024]{1,0:T(8,128)(2,1)}) %tuple.146), branch_computations={%region_5.0_spmd, %region_6.0_spmd} | conditional | flops 4297064448 | bytes 17825810 | solution.py:85
  191.9 10.1 %convolution_convert_fusion.5 = bf16[512,1024]{1,0:T(8,128)(2,1)} fusion(bf16[512,4096]{1,0:T(8,128)(2,1)} %get-tuple-element.113, bf16[4096,1024]{1,0:T(8,128)(2,1)} %get-tuple-element.114), kind=kOutput, calls=%fused_computation.5 | convolution fusion | flops 4295491584 | bytes 13631488 | tf_op jit(solution)/shard_map/phase_a/cond/branch_1_fun/dot_general | solution.py:76
  210.4 13.5 %conditional.16 = (bf16[512,1024]{1,0:T(8,128)(2,1)S(1)}, f32[512,4096]{1,0:T(8,128)}) conditional(s32[]{:T(128)} %convert_element_type.174, (bf16[512,1024]{1,0:T(8,128)(2,1)S(1)}, bf16[4096,1024]{1,0:T(8,128)(2,1)}) %tuple.147, (bf16[512,4096]{1,0:T(8,128)(2,1)}, bf16[4096,1024]{1,0:T(8,128)(2,1)}) %tuple.148), branch_computations={%region_7.0_spmd, %region_8.0_spmd} | conditional | flops 4299161600 | bytes 22020116 | solution.py:85
  210.4 9.1 %convolution_convert_fusion.7 = bf16[512,1024]{1,0:T(8,128)(2,1)S(1)} fusion(bf16[512,4096]{1,0:T(8,128)(2,1)} %get-tuple-element.117, bf16[4096,1024]{1,0:T(8,128)(2,1)} %get-tuple-element.118), kind=kOutput, calls=%fused_computation.8 | convolution fusion | flops 4295491584 | bytes 13631488 | tf_op jit(solution)/shard_map/phase_a/cond/branch_1_fun/dot_general | solution.py:76
  233.1 9.9 %abs_reduce_fusion.1 = (f32[8,4096]{1,0:T(8,128)S(1)}, f32[8,64,4096]{2,1,0:T(8,128)}) fusion(f32[8,4096]{1,0:T(8,128)S(1)} %broadcast_bitcast_fusion.4, s32[1,2,8,64,4096]{4,3,2,1,0:T(8,128)} %param.25, bf16[8,64,4096]{2,1,0:T(8,128)(2,1)S(1)} %copy-done.2, f32[8,4096]{1,0:T(8,128)S(1)} %broadcast_bitcast_fusion.5, ...), kind=kLoop, calls=%fused_computation.99 | loop fusion | flops 23035904 | bytes 33947648 | tf_op jit(solution)/shard_map/phase_a/reduce_max | solution.py:128
  243.1 15.9 %pmax.14 = f32[8,32]{0,1:T(8,128)S(1)} all-reduce(f32[8,32]{0,1:T(8,128)S(1)} %bitcast_reduce_fusion.1), channel_id=1, replica_groups=mesh['dp'=4,'section'=2,'tensor'=4] {'tensor'}, use_global_device_ids=true, to_apply=%region_11.0 | all-reduce | flops 256 | bytes 2048 | tf_op jit(solution)/shard_map/phase_a/pmax | solution.py:129
  259.2 9.0 %multiply_convert_fusion.1 = bf16[8,64,4096]{2,1,0:T(8,128)(2,1)S(1)} fusion(f32[8,64,4096]{2,1,0:T(8,128)} %get-tuple-element.191, f32[8,4096]{1,0:T(8,128)S(1)} %get-tuple-element.210, f32[8,4096]{1,0:T(8,128)S(1)} %get-tuple-element.211), kind=kLoop, calls=%fused_computation.89 | loop fusion | flops 56623104 | bytes 12845056 | tf_op jit(solution)/shard_map/phase_a/convert_element_type | solution.py:134
  271.6 10.5 %add_convert_fusion.1 = bf16[512,4096]{1,0:T(8,128)(2,1)} fusion(f32[512,4096]{1,0:T(8,128)} %get-tuple-element.177, bf16[512,4096]{1,0:T(8,128)(2,1)} %collective-permute-done.12, bf16[512,4096]{1,0:T(8,128)(2,1)} %collective-permute-done.11, bf16[512,4096]{1,0:T(8,128)(2,1)} %collective-permute-done.10), kind=kLoop, calls=%fused_computation.86 | loop fusion | flops 14680064 | bytes 25165824 | tf_op jit(solution)/shard_map/phase_a/convert_element_type | solution.py:138
  310.7 34.6 %collective-permute-done.13 = bf16[8,64,4096]{2,1,0:T(8,128)(2,1)S(1)} collective-permute-done((bf16[8,64,4096]{2,1,0:T(8,128)(2,1)S(1)}, bf16[8,64,4096]{2,1,0:T(8,128)(2,1)S(1)}, u32[]{:S(2)}, u32[]{:S(2)}) %collective-permute-start.13) | collective-permute-done | bytes 4194336 | tf_op jit(solution)/shard_map/phase_a/ppermute | solution.py:162
  357.1 18.8 %collective-permute-done.14 = bf16[512,1024]{1,0:T(8,128)(2,1)} collective-permute-done((bf16[512,1024]{1,0:T(8,128)(2,1)S(1)}, bf16[512,1024]{1,0:T(8,128)(2,1)}, u32[]{:S(2)}, u32[]{:S(2)}) %collective-permute-start.14) | collective-permute-done | bytes 1048608 | tf_op jit(solution)/shard_map/phase_a/ppermute | solution.py:59
  379.9 19.3 %collective-permute-done.20 = bf16[512,1024]{1,0:T(8,128)(2,1)} collective-permute-done((bf16[512,1024]{1,0:T(8,128)(2,1)S(1)}, bf16[512,1024]{1,0:T(8,128)(2,1)}, u32[]{:S(2)}, u32[]{:S(2)}) %collective-permute-start.20) | collective-permute-done | bytes 1048608 | tf_op jit(solution)/shard_map/phase_a/ppermute | solution.py:59
  399.3 24.0 %conditional.21 = (bf16[4096,1024]{1,0:T(8,128)(2,1)}) conditional(s32[]{:T(128)} %convert_element_type.174, (bf16[512,4096]{1,0:T(8,128)(2,1)}, bf16[512,4096]{1,0:T(8,128)(2,1)}, bf16[512,4096]{1,0:T(8,128)(2,1)}, bf16[512,4096]{1,0:T(8,128)(2,1)}, bf16[512,1024]{1,0:T(8,128)(2,1)S(1)}, /*index=5*/bf16[512,1024]{1,0:T(8,128)(2,1)}, ...), branch_computations={%region_26.27_spmd, %region_27.28_spmd} | conditional | flops 17263755264 | bytes 29360136
  399.5 23.8 %fusion.18 = bf16[4096,1024]{1,0:T(8,128)(2,1)} fusion(bf16[512,4096]{1,0:T(8,128)(2,1)} %get-tuple-element.146, bf16[512,4096]{1,0:T(8,128)(2,1)} %get-tuple-element.145, bf16[512,4096]{1,0:T(8,128)(2,1)} %get-tuple-element.144, bf16[512,4096]{1,0:T(8,128)(2,1)} %get-tuple-element.143, bf16[512,1024]{1,0:T(8,128)(2,1)} %get-tuple-element.150, ...), kind=kOutput, calls=%fused_computation.34 | convolution fusion | flops 17263755264 | bytes 29360128 | tf_op jit(solution)/shard_map/weight_grad/cond/branch_1_fun/dot_general | solution.py:169
  423.3 10.8 %conditional.17 = (bf16[512,1024]{1,0:T(8,128)(2,1)S(1)}, bf16[512,4096]{1,0:T(8,128)(2,1)}) conditional(s32[]{:T(128)} %convert_element_type.182, (bf16[512,1024]{1,0:T(8,128)(2,1)}, bf16[4096,1024]{1,0:T(8,128)(2,1)}) %tuple.149, (bf16[512,4096]{1,0:T(8,128)(2,1)}, bf16[4096,1024]{1,0:T(8,128)(2,1)}) %tuple.150), branch_computations={%region_14.15_spmd, %region_15.16_spmd} | conditional | flops 4297064448 | bytes 17825810 | solution.py:85
  423.7 10.2 %convolution_convert_fusion.8 = bf16[512,4096]{1,0:T(8,128)(2,1)} fusion(bf16[512,1024]{1,0:T(8,128)(2,1)} %get-tuple-element.119, bf16[4096,1024]{1,0:T(8,128)(2,1)} %get-tuple-element.120), kind=kOutput, calls=%fused_computation.9 | convolution fusion | flops 4297064448 | bytes 13631488 | tf_op jit(solution)/shard_map/phase_b/cond/branch_0_fun/dot_general | solution.py:80
  436.6 10.6 %conditional.18 = (bf16[512,1024]{1,0:T(8,128)(2,1)S(1)}, bf16[512,4096]{1,0:T(8,128)(2,1)}) conditional(s32[]{:T(128)} %convert_element_type.182, (bf16[512,1024]{1,0:T(8,128)(2,1)}, bf16[4096,1024]{1,0:T(8,128)(2,1)}) %tuple.151, (bf16[512,4096]{1,0:T(8,128)(2,1)}, bf16[4096,1024]{1,0:T(8,128)(2,1)}) %tuple.152), branch_computations={%region_16.17_spmd, %region_17.18_spmd} | conditional | flops 4297064448 | bytes 17825810 | solution.py:85
  436.6 10.3 %convolution_convert_fusion.10 = bf16[512,4096]{1,0:T(8,128)(2,1)} fusion(bf16[512,1024]{1,0:T(8,128)(2,1)} %get-tuple-element.123, bf16[4096,1024]{1,0:T(8,128)(2,1)} %get-tuple-element.124), kind=kOutput, calls=%fused_computation.11 | convolution fusion | flops 4297064448 | bytes 13631488 | tf_op jit(solution)/shard_map/phase_b/cond/branch_0_fun/dot_general | solution.py:80
  449.7 11.4 %conditional.19 = (bf16[512,1024]{1,0:T(8,128)(2,1)}, bf16[512,4096]{1,0:T(8,128)(2,1)}) conditional(s32[]{:T(128)} %convert_element_type.182, (bf16[512,1024]{1,0:T(8,128)(2,1)}, bf16[4096,1024]{1,0:T(8,128)(2,1)}) %tuple.153, (bf16[512,4096]{1,0:T(8,128)(2,1)}, bf16[4096,1024]{1,0:T(8,128)(2,1)}) %tuple.154), branch_computations={%region_18.19_spmd, %region_19.20_spmd} | conditional | flops 4297064448 | bytes 17825810 | solution.py:85
  449.7 10.3 %convolution_convert_fusion.12 = bf16[512,4096]{1,0:T(8,128)(2,1)} fusion(bf16[512,1024]{1,0:T(8,128)(2,1)} %get-tuple-element.127, bf16[4096,1024]{1,0:T(8,128)(2,1)} %get-tuple-element.128), kind=kOutput, calls=%fused_computation.13 | convolution fusion | flops 4297064448 | bytes 13631488 | tf_op jit(solution)/shard_map/phase_b/cond/branch_0_fun/dot_general | solution.py:80
  467.9 10.4 %conditional.20 = (bf16[512,1024]{1,0:T(8,128)(2,1)S(1)}, f32[512,4096]{1,0:T(8,128)}) conditional(s32[]{:T(128)} %convert_element_type.182, (bf16[512,1024]{1,0:T(8,128)(2,1)S(1)}, bf16[4096,1024]{1,0:T(8,128)(2,1)}) %tuple.155, (bf16[512,4096]{1,0:T(8,128)(2,1)}, bf16[4096,1024]{1,0:T(8,128)(2,1)}) %tuple.156), branch_computations={%region_20.21_spmd, %region_21.22_spmd} | conditional | flops 4299161600 | bytes 22020116 | solution.py:85
  468.1 10.1 %fusion.1 = f32[512,4096]{1,0:T(8,128)} fusion(bf16[512,1024]{1,0:T(8,128)(2,1)S(1)} %get-tuple-element.131, bf16[4096,1024]{1,0:T(8,128)(2,1)} %get-tuple-element.132), kind=kOutput, calls=%fused_computation.16 | convolution fusion | flops 4299161600 | bytes 17825792 | tf_op jit(solution)/shard_map/phase_b/cond/branch_0_fun/dot_general | solution.py:80
  480.6 20.4 %collective-permute-done.23 = bf16[512,4096]{1,0:T(8,128)(2,1)} collective-permute-done((bf16[512,4096]{1,0:T(8,128)(2,1)}, bf16[512,4096]{1,0:T(8,128)(2,1)}, u32[]{:S(2)}, u32[]{:S(2)}) %collective-permute-start.23) | collective-permute-done | bytes 4194336 | tf_op jit(solution)/shard_map/phase_b/ppermute | solution.py:66
  501.1 55.2 %collective-permute-done.24 = bf16[512,4096]{1,0:T(8,128)(2,1)} collective-permute-done((bf16[512,4096]{1,0:T(8,128)(2,1)}, bf16[512,4096]{1,0:T(8,128)(2,1)}, u32[]{:S(2)}, u32[]{:S(2)}) %collective-permute-start.24) | collective-permute-done | bytes 4194336 | tf_op jit(solution)/shard_map/phase_b/ppermute | solution.py:66
  556.3 8.6 %add_convert_fusion = bf16[512,4096]{1,0:T(8,128)(2,1)S(1)} fusion(f32[512,4096]{1,0:T(8,128)} %get-tuple-element.185, bf16[512,4096]{1,0:T(8,128)(2,1)} %collective-permute-done.25, bf16[512,4096]{1,0:T(8,128)(2,1)} %collective-permute-done.24, bf16[512,4096]{1,0:T(8,128)(2,1)} %collective-permute-done.23), kind=kLoop, calls=%fused_computation.74 | loop fusion | flops 14680064 | bytes 25165824 | tf_op jit(solution)/shard_map/phase_b/convert_element_type | solution.py:138
  572.1 18.0 %pmax.15 = f32[8,32]{0,1:T(8,128)S(1)} all-reduce(f32[8,32]{0,1:T(8,128)S(1)} %bitcast_reduce_fusion), channel_id=1, replica_groups=mesh['dp'=4,'section'=2,'tensor'=4] {'tensor'}, use_global_device_ids=true, to_apply=%region_24.25 | all-reduce | flops 256 | bytes 2048 | tf_op jit(solution)/shard_map/phase_b/pmax | solution.py:129
  590.4 23.9 %fusion.58 = (bf16[1,8,64,4096]{3,2,1,0:T(8,128)(2,1)}, bf16[1,8,64,4096]{3,2,1,0:T(8,128)(2,1)}) fusion(bf16[8,64,4096]{2,1,0:T(8,128)(2,1)} %copy-done.6, f32[8,64,4096]{2,1,0:T(8,128)} %copy-done, bf16[8,64,4096]{2,1,0:T(8,128)(2,1)} %copy-done.8, f32[8,64]{1,0:T(8,128)S(1)} %broadcast_multiply_fusion, f32[8,64]{1,0:T(8,128)S(1)} %copy-done.18, ...), kind=kLoop, calls=%fused_computation.106 | loop fusion | flops 144703488 | bytes 50991104 | tf_op jit(solution)/shard_map/broadcast_in_dim | solution.py:195
  614.3 25.2 %reduce-scatter.2.cloned.1.call-done = bf16[1024,1024]{1,0:T(8,128)(2,1)} async-done(((bf16[4096,1024]{1,0:T(8,128)(2,1)}), bf16[1024,1024]{1,0:T(8,128)(2,1)}) %reduce-scatter.2.cloned.1.call-update) | async-done | bytes 2097168 | tf_op jit(solution)/shard_map/weight_grad/reduce_scatter | solution.py:182
  (155 shorter events, 139.8 us)
Async XLA Ops:
  7.2 155.7 %all-gather.3.cloned.1.call-start = ((), (), s32[]{:S(2)}) async-start(), calls=%async_computation.2 | async-start | bytes 10485760 | tf_op jit(solution)/shard_map/all_gather | solution.py:71
  10.3 629.1 %reduce-scatter.2.cloned.1.call-start = ((), (), s32[]{:S(2)}) async-start(), calls=%async_computation.1 | async-start | bytes 10485760 | tf_op jit(solution)/shard_map/weight_grad/reduce_scatter | solution.py:182
  23.1 139.7 %collective-permute-start.1 = (bf16[512,4096]{1,0:T(8,128)(2,1)}, bf16[512,4096]{1,0:T(8,128)(2,1)}, u32[]{:S(2)}, u32[]{:S(2)}) collective-permute-start(bf16[512,4096]{1,0:T(8,128)(2,1)} %bitcast.5), channel_id=1, source_target_pairs={{0,8},{8,0},{16,24},{24,16},{1,9},{9,1},{17,25},{25,17},{2,10},{10... | collective-permute-start | bytes 12582920 | tf_op jit(solution)/shard_map/phase_a/ppermute | solution.py:59
  28.5 148.6 %collective-permute-start.4 = (bf16[512,4096]{1,0:T(8,128)(2,1)}, bf16[512,4096]{1,0:T(8,128)(2,1)}, u32[]{:S(2)}, u32[]{:S(2)}) collective-permute-start(bf16[512,4096]{1,0:T(8,128)(2,1)} %bitcast.5), channel_id=1, source_target_pairs={{0,16},{8,24},{16,0},{24,8},{1,17},{9,25},{17,1},{25,9},{2,18},{10... | collective-permute-start | bytes 12582920 | tf_op jit(solution)/shard_map/phase_a/ppermute | solution.py:59
  31.9 159.5 %collective-permute-start.7 = (bf16[512,4096]{1,0:T(8,128)(2,1)}, bf16[512,4096]{1,0:T(8,128)(2,1)}, u32[]{:S(2)}, u32[]{:S(2)}) collective-permute-start(bf16[512,4096]{1,0:T(8,128)(2,1)} %bitcast.5), channel_id=1, source_target_pairs={{0,24},{8,16},{16,8},{24,0},{1,25},{9,17},{17,9},{25,1},{2,26},{10... | collective-permute-start | bytes 12582920 | tf_op jit(solution)/shard_map/phase_a/ppermute | solution.py:59
  37.7 2.4 collective-permute-start
  38.4 138.6 %collective-permute-start.3 = (bf16[512,1024]{1,0:T(8,128)(2,1)}, bf16[512,1024]{1,0:T(8,128)(2,1)}, u32[]{:S(2)}, u32[]{:S(2)}) collective-permute-start(bf16[512,1024]{1,0:T(8,128)(2,1)} %get-tuple-element.202), channel_id=1, source_target_pairs={{4,20},{12,28},{20,4},{28,12},{5,21},{13,29},{21,5},{29,13},{6,22}... | collective-permute-start | bytes 3145736 | tf_op jit(solution)/shard_map/phase_a/ppermute | solution.py:59
  41.1 150.3 %collective-permute-start.6 = (bf16[512,1024]{1,0:T(8,128)(2,1)S(1)}, bf16[512,1024]{1,0:T(8,128)(2,1)}, u32[]{:S(2)}, u32[]{:S(2)}) collective-permute-start(bf16[512,1024]{1,0:T(8,128)(2,1)S(1)} %get-tuple-element.201), channel_id=1, source_target_pairs={{4,28},{12,20},{20,12},{28,4},{5,29},{13,21},{21,13},{29,5},{6,30}... | collective-permute-start | bytes 3145736 | tf_op jit(solution)/shard_map/phase_a/ppermute | solution.py:59
  173.6 50.3 %collective-permute-start.2 = (bf16[512,1024]{1,0:T(8,128)(2,1)}, bf16[512,1024]{1,0:T(8,128)(2,1)}, u32[]{:S(2)}, u32[]{:S(2)}) collective-permute-start(bf16[512,1024]{1,0:T(8,128)(2,1)} %get-tuple-element.170), channel_id=1, source_target_pairs={{0,8},{8,0},{16,24},{24,16},{1,9},{9,1},{17,25},{25,17},{2,10},{10... | collective-permute-start | bytes 3145736 | tf_op jit(solution)/shard_map/phase_a/ppermute | solution.py:66
  188.0 40.8 %collective-permute-start.5 = (bf16[512,1024]{1,0:T(8,128)(2,1)}, bf16[512,1024]{1,0:T(8,128)(2,1)}, u32[]{:S(2)}, u32[]{:S(2)}) collective-permute-start(bf16[512,1024]{1,0:T(8,128)(2,1)} %get-tuple-element.171), channel_id=1, source_target_pairs={{0,16},{8,24},{16,0},{24,8},{1,17},{9,25},{17,1},{25,9},{2,18},{10... | collective-permute-start | bytes 3145736 | tf_op jit(solution)/shard_map/phase_a/ppermute | solution.py:66
  202.5 29.1 %collective-permute-start.8 = (bf16[512,1024]{1,0:T(8,128)(2,1)}, bf16[512,1024]{1,0:T(8,128)(2,1)}, u32[]{:S(2)}, u32[]{:S(2)}) collective-permute-start(bf16[512,1024]{1,0:T(8,128)(2,1)} %get-tuple-element.172), channel_id=1, source_target_pairs={{0,24},{8,16},{16,8},{24,0},{1,25},{9,17},{17,9},{25,1},{2,26},{10... | collective-permute-start | bytes 3145736 | tf_op jit(solution)/shard_map/phase_a/ppermute | solution.py:66
  205.1 28.0 %copy-start.9 = (f32[8,4096]{1,0:T(8,128)}, f32[8,4096]{1,0:T(8,128)S(1)}, u32[]{:S(2)}) copy-start(f32[8,4096]{1,0:T(8,128)S(1)} %broadcast_bitcast_fusion.4) | copy-start | bytes 393220
  205.1 66.5 %collective-permute-start.10 = (bf16[512,4096]{1,0:T(8,128)(2,1)}, bf16[512,4096]{1,0:T(8,128)(2,1)}, u32[]{:S(2)}, u32[]{:S(2)}) collective-permute-start(bf16[512,4096]{1,0:T(8,128)(2,1)} %copy-done.19), channel_id=1, source_target_pairs={{4,12},{12,4},{20,28},{28,20},{5,13},{13,5},{21,29},{29,21},{6,14}... | collective-permute-start | bytes 12582920 | tf_op jit(solution)/shard_map/phase_a/ppermute | solution.py:66
  207.7 63.9 %collective-permute-start.11 = (bf16[512,4096]{1,0:T(8,128)(2,1)}, bf16[512,4096]{1,0:T(8,128)(2,1)}, u32[]{:S(2)}, u32[]{:S(2)}) collective-permute-start(bf16[512,4096]{1,0:T(8,128)(2,1)} %copy-done.20), channel_id=1, source_target_pairs={{4,20},{12,28},{20,4},{28,12},{5,21},{13,29},{21,5},{29,13},{6,22}... | collective-permute-start | bytes 12582920 | tf_op jit(solution)/shard_map/phase_a/ppermute | solution.py:66
  223.9 47.6 %collective-permute-start.12 = (bf16[512,4096]{1,0:T(8,128)(2,1)}, bf16[512,4096]{1,0:T(8,128)(2,1)}, u32[]{:S(2)}, u32[]{:S(2)}) collective-permute-start(bf16[512,4096]{1,0:T(8,128)(2,1)} %copy-done.21), channel_id=1, source_target_pairs={{4,28},{12,20},{20,12},{28,4},{5,29},{13,21},{21,13},{29,5},{6,30}... | collective-permute-start | bytes 12582920 | tf_op jit(solution)/shard_map/phase_a/ppermute | solution.py:66
  268.3 13.8 %collective-permute-start.9 = (bf16[8,64,4096]{2,1,0:T(8,128)(2,1)S(1)}, bf16[8,64,4096]{2,1,0:T(8,128)(2,1)}, u32[]{:S(2)}, u32[]{:S(2)}) collective-permute-start(bf16[8,64,4096]{2,1,0:T(8,128)(2,1)S(1)} %multiply_convert_fusion.1), channel_id=1, source_target_pairs={{0,4},{1,5},{2,6},{3,7},{8,12},{9,13},{10,14},{11,15},{16,20},{17,... | collective-permute-start | bytes 12582920 | tf_op jit(solution)/shard_map/phase_a/ppermute | solution.py:157
  301.4 43.9 %collective-permute-start.13 = (bf16[8,64,4096]{2,1,0:T(8,128)(2,1)S(1)}, bf16[8,64,4096]{2,1,0:T(8,128)(2,1)S(1)}, u32[]{:S(2)}, u32[]{:S(2)}) collective-permute-start(bf16[8,64,4096]{2,1,0:T(8,128)(2,1)S(1)} %fusion.37), channel_id=1, source_target_pairs={{4,0},{5,1},{6,2},{7,3},{12,8},{13,9},{14,10},{15,11},{20,16},{21,... | collective-permute-start | bytes 12582920 | tf_op jit(solution)/shard_map/phase_a/ppermute | solution.py:162
  302.7 51.1 %collective-permute-start.15 = (bf16[512,4096]{1,0:T(8,128)(2,1)}, bf16[512,4096]{1,0:T(8,128)(2,1)}, u32[]{:S(2)}, u32[]{:S(2)}) collective-permute-start(bf16[512,4096]{1,0:T(8,128)(2,1)} %bitcast.16), channel_id=1, source_target_pairs={{4,12},{12,4},{20,28},{28,20},{5,13},{13,5},{21,29},{29,21},{6,14}... | collective-permute-start | bytes 12582920 | tf_op jit(solution)/shard_map/phase_a/ppermute | solution.py:59
  305.4 51.7 %collective-permute-start.18 = (bf16[512,4096]{1,0:T(8,128)(2,1)}, bf16[512,4096]{1,0:T(8,128)(2,1)}, u32[]{:S(2)}, u32[]{:S(2)}) collective-permute-start(bf16[512,4096]{1,0:T(8,128)(2,1)} %bitcast.16), channel_id=1, source_target_pairs={{4,20},{12,28},{20,4},{28,12},{5,21},{13,29},{21,5},{29,13},{6,22}... | collective-permute-start | bytes 12582920 | tf_op jit(solution)/shard_map/phase_a/ppermute | solution.py:59
  308.0 49.1 %collective-permute-start.21 = (bf16[512,4096]{1,0:T(8,128)(2,1)}, bf16[512,4096]{1,0:T(8,128)(2,1)}, u32[]{:S(2)}, u32[]{:S(2)}) collective-permute-start(bf16[512,4096]{1,0:T(8,128)(2,1)} %bitcast.16), channel_id=1, source_target_pairs={{4,28},{12,20},{20,12},{28,4},{5,29},{13,21},{21,13},{29,5},{6,30}... | collective-permute-start | bytes 12582920 | tf_op jit(solution)/shard_map/phase_a/ppermute | solution.py:59
  347.8 28.0 %collective-permute-start.14 = (bf16[512,1024]{1,0:T(8,128)(2,1)S(1)}, bf16[512,1024]{1,0:T(8,128)(2,1)}, u32[]{:S(2)}, u32[]{:S(2)}) collective-permute-start(bf16[512,1024]{1,0:T(8,128)(2,1)S(1)} %get-tuple-element.196), channel_id=1, source_target_pairs={{0,8},{8,0},{16,24},{24,16},{1,9},{9,1},{17,25},{25,17},{2,10},{10... | collective-permute-start | bytes 3145736 | tf_op jit(solution)/shard_map/phase_a/ppermute | solution.py:59
  350.3 29.6 %collective-permute-start.17 = (bf16[512,1024]{1,0:T(8,128)(2,1)S(1)}, bf16[512,1024]{1,0:T(8,128)(2,1)}, u32[]{:S(2)}, u32[]{:S(2)}) collective-permute-start(bf16[512,1024]{1,0:T(8,128)(2,1)S(1)} %get-tuple-element.199), channel_id=1, source_target_pairs={{0,16},{8,24},{16,0},{24,8},{1,17},{9,25},{17,1},{25,9},{2,18},{10... | collective-permute-start | bytes 3145736 | tf_op jit(solution)/shard_map/phase_a/ppermute | solution.py:59
  353.7 45.5 %collective-permute-start.20 = (bf16[512,1024]{1,0:T(8,128)(2,1)S(1)}, bf16[512,1024]{1,0:T(8,128)(2,1)}, u32[]{:S(2)}, u32[]{:S(2)}) collective-permute-start(bf16[512,1024]{1,0:T(8,128)(2,1)S(1)} %get-tuple-element.198), channel_id=1, source_target_pairs={{0,24},{8,16},{16,8},{24,0},{1,25},{9,17},{17,9},{25,1},{2,26},{10... | collective-permute-start | bytes 3145736 | tf_op jit(solution)/shard_map/phase_a/ppermute | solution.py:59
  434.1 67.0 %collective-permute-start.23 = (bf16[512,4096]{1,0:T(8,128)(2,1)}, bf16[512,4096]{1,0:T(8,128)(2,1)}, u32[]{:S(2)}, u32[]{:S(2)}) collective-permute-start(bf16[512,4096]{1,0:T(8,128)(2,1)} %get-tuple-element.182), channel_id=1, source_target_pairs={{0,8},{8,0},{16,24},{24,16},{1,9},{9,1},{17,25},{25,17},{2,10},{10... | collective-permute-start | bytes 12582920 | tf_op jit(solution)/shard_map/phase_b/ppermute | solution.py:66
  447.2 109.1 %collective-permute-start.24 = (bf16[512,4096]{1,0:T(8,128)(2,1)}, bf16[512,4096]{1,0:T(8,128)(2,1)}, u32[]{:S(2)}, u32[]{:S(2)}) collective-permute-start(bf16[512,4096]{1,0:T(8,128)(2,1)} %get-tuple-element.183), channel_id=1, source_target_pairs={{0,16},{8,24},{16,0},{24,8},{1,17},{9,25},{17,1},{25,9},{2,18},{10... | collective-permute-start | bytes 12582920 | tf_op jit(solution)/shard_map/phase_b/ppermute | solution.py:66
  461.1 95.2 %collective-permute-start.25 = (bf16[512,4096]{1,0:T(8,128)(2,1)}, bf16[512,4096]{1,0:T(8,128)(2,1)}, u32[]{:S(2)}, u32[]{:S(2)}) collective-permute-start(bf16[512,4096]{1,0:T(8,128)(2,1)} %get-tuple-element.184), channel_id=1, source_target_pairs={{0,24},{8,16},{16,8},{24,0},{1,25},{9,17},{17,9},{25,1},{2,26},{10... | collective-permute-start | bytes 12582920 | tf_op jit(solution)/shard_map/phase_b/ppermute | solution.py:66
  465.4 1.5 collective-permute-start.16
  466.1 14.0 %collective-permute-start.19 = (bf16[512,1024]{1,0:T(8,128)(2,1)}, bf16[512,1024]{1,0:T(8,128)(2,1)S(1)}, u32[]{:S(2)}, u32[]{:S(2)}) collective-permute-start(bf16[512,1024]{1,0:T(8,128)(2,1)} %copy-done.16), channel_id=1, source_target_pairs={{4,20},{12,28},{20,4},{28,12},{5,21},{13,29},{21,5},{29,13},{6,22}... | collective-permute-start | bytes 3145736 | tf_op jit(solution)/shard_map/phase_b/ppermute | solution.py:66
  466.9 13.4 %collective-permute-start.22 = (bf16[512,1024]{1,0:T(8,128)(2,1)}, bf16[512,1024]{1,0:T(8,128)(2,1)S(1)}, u32[]{:S(2)}, u32[]{:S(2)}) collective-permute-start(bf16[512,1024]{1,0:T(8,128)(2,1)} %get-tuple-element.180), channel_id=1, source_target_pairs={{4,28},{12,20},{20,12},{28,4},{5,29},{13,21},{21,13},{29,5},{6,30}... | collective-permute-start | bytes 3145736 | tf_op jit(solution)/shard_map/phase_b/ppermute | solution.py:66
  480.3 84.7 %slice-start = ((s8[8388608]{0:T(1024)(128)(4,1)}), s8[4194304]{0:T(1024)(128)(4,1)S(1)}, s32[]{:S(2)}) async-start(s8[8388608]{0:T(1024)(128)(4,1)} %bitcast.100), calls=%async_computation.3 | async-start | bytes 8388608
  480.6 84.4 %copy-start.3 = (bf16[512,4096]{1,0:T(8,128)(2,1)}, bf16[512,4096]{1,0:T(8,128)(2,1)S(1)}, u32[]{:S(2)}) copy-start(bf16[512,4096]{1,0:T(8,128)(2,1)S(1)} %constant_dynamic-update-slice_fusion) | copy-start | bytes 12582916
  565.0 25.3 %copy-start.12 = (f32[8,4096]{1,0:T(8,128)S(1)}, f32[8,4096]{1,0:T(8,128)}, u32[]{:S(2)}) copy-start(f32[8,4096]{1,0:T(8,128)} %copy-done.11) | copy-start | bytes 393220
  (25 other events, 241.4 us)
Sparse Core Ops, SparseCore 0:
  10.4 152.3 all-gather.2
  423.4 216.0 reduce-scatter.1
where the time goes:
time: 660 us; the launch traced here: 651 us
  waiting for transfers between devices  299 us (45%)
  matrix products  104 us (16%)
  other arithmetic  101 us (15%)
  starting transfers between devices  65.6 us (10%)
  blocking collectives  33.9 us (5%)
  local copies, waits for them, and re-layouts  29.3 us (4%)
  between operations  15.3 us (2%)
    all_gather x1, waiting for transfers between devices, local(): lax.all_gather(columns(weight[0], replica), 'tensor', axis=0, tiled=True)  120 us
    ppermute x12, waiting for transfers between devices, give_back(): return lax.ppermute(value, ('dp', 'section'), pairs)  77.2 us
    ppermute x12, waiting for transfers between devices, exchange(): return lax.ppermute(value, ('dp', 'section'), pairs)  42.2 us
    dot_general x4, matrix products, backward(): lax.dot_general(piece, weight_part, (((1,), (1,)), ((), ())), preferred_e...  40.9 us
    dot_general x4, matrix products, forward(): out = jnp.dot(whole, weight_part, preferred_element_type=f32).astype(bf16)  39.7 us
    ppermute x1, waiting for transfers between devices, local(): upstream = lax.ppermute(grads[c], 'section', [(1, 0)])  34.6 us
    pmax x2, blocking collectives, finish_forward(): spread = lax.pmax(peak, 'tensor') + epsilon  33.9 us
    ppermute x12, starting transfers between devices, exchange(): return lax.ppermute(value, ('dp', 'section'), pairs)  32.1 us
  transfers between devices with their start and end apart: 28, of which 9 were waited for; matrix products, arithmetic and copies ran while one was open for 28% of the time, Pallas kernels for 0%

commit v1 on v0

--- a/solution.py
+++ b/solution.py
@@ -68,7 +68,9 @@
     def columns(value, index):
         return lax.dynamic_slice_in_dim(value, index * part, part, 1)
 
-    weight_part = lax.all_gather(columns(weight[0], replica), "tensor", axis=0, tiled=True)
+    own = columns(weight[0], replica)
+    stack = jnp.stack([own] * lax.axis_size("tensor"))
+    weight_part = jnp.concatenate(lax.all_to_all(stack, "tensor", 0, 0), axis=0)
 
     def product(forward_here, whole, piece):
 

time: 660 us -> 703 us (1.065)
  waiting for transfers between devices: 299 us -> 331 us
    all_to_all x0 -> x1, waiting for transfers between devices: none -> 154 us  [local(): weight_part = jnp.concatenate(lax.all_to_all(stack, 'tensor', 0, 0), axis=0)]
    all_gather x1 -> x0, waiting for transfers between devices: 120 us -> none  [local(): lax.all_gather(columns(weight[0], replica), 'tensor', axis=0, tiled=True)]
    another operation x10 -> x12, local copies, waits for them, and re-layouts: 8.33 us -> 16.5 us
  transfers between devices with their start and end apart: 28 -> 28, of which waited for: 9 -> 9; matrix products, arithmetic and copies ran while one was open for 28% -> 26% of each run, Pallas kernels for 0% -> 0%
where the time goes in v1:
time: 703 us; the launch traced here: 694 us
  waiting for transfers between devices  331 us (47%)
  matrix products  104 us (15%)
  other arithmetic  100 us (14%)
  starting transfers between devices  70.8 us (10%)
  blocking collectives  36 us (5%)
  local copies, waits for them, and re-layouts  34.4 us (5%)
  between operations  15.3 us (2%)
    all_to_all x1, waiting for transfers between devices, local(): weight_part = jnp.concatenate(lax.all_to_all(stack, 'tensor', 0, 0), axis=0)  154 us
    ppermute x12, waiting for transfers between devices, give_back(): return lax.ppermute(value, ('dp', 'section'), pairs)  77.3 us
    ppermute x12, waiting for transfers between devices, exchange(): return lax.ppermute(value, ('dp', 'section'), pairs)  42 us
    dot_general x4, matrix products, backward(): lax.dot_general(piece, weight_part, (((1,), (1,)), ((), ())), preferred_e...  40.9 us
    dot_general x4, matrix products, forward(): out = jnp.dot(whole, weight_part, preferred_element_type=f32).astype(bf16)  39.7 us
    pmax x2, blocking collectives, finish_forward(): spread = lax.pmax(peak, 'tensor') + epsilon  36 us
    ppermute x1, waiting for transfers between devices, local(): upstream = lax.ppermute(grads[c], 'section', [(1, 0)])  32.4 us
    ppermute x12, starting transfers between devices, exchange(): return lax.ppermute(value, ('dp', 'section'), pairs)  30.9 us
  transfers between devices with their start and end apart: 28, of which 9 were waited for; matrix products, arithmetic and copies ran while one was open for 26% of the time, Pallas kernels for 0%

profile of v1, /device:TPU:0, one launch (start us, length us, event | category | flops | bytes accessed | tf_op | source)
XLA Modules:
  0.0 694.1 jit_solution(12847464152657061611)
XLA Ops:
  49.9 154.0 %all-to-all-done = bf16[4,1024,1024]{2,1,0:T(8,128)(2,1)} async-done(((bf16[4,1024,1024]{2,1,0:T(8,128)(2,1)}), bf16[4,1024,1024]{2,1,0:T(8,128)(2,1)}, u32[]{:S(2)}, u32[]{:S(2)}) %all-to-all-start) | async-done | bytes 8388640 | tf_op jit(solution)/shard_map/all_to_all | solution.py:73
  203.9 10.8 %conditional.13 = (bf16[512,1024]{1,0:T(8,128)(2,1)}, bf16[512,4096]{1,0:T(8,128)(2,1)S(1)}) conditional(s32[]{:T(128)} %convert_element_type.174, (bf16[512,1024]{1,0:T(8,128)(2,1)}, bf16[4096,1024]{1,0:T(8,128)(2,1)}) %tuple.139, (bf16[512,4096]{1,0:T(8,128)(2,1)}, bf16[4096,1024]{1,0:T(8,128)(2,1)}) %tuple.86), branch_computations={%region_1.0_spmd, %region_2.0_spmd} | conditional | flops 4297064448 | bytes 17825810 | solution.py:87
  203.9 10.3 %convolution_convert_fusion.1 = bf16[512,1024]{1,0:T(8,128)(2,1)} fusion(bf16[512,4096]{1,0:T(8,128)(2,1)} %get-tuple-element.105, bf16[4096,1024]{1,0:T(8,128)(2,1)} %get-tuple-element.106), kind=kOutput, calls=%fused_computation.1 | convolution fusion | flops 4295491584 | bytes 13631488 | tf_op jit(solution)/shard_map/phase_a/cond/branch_1_fun/dot_general | solution.py:78
  218.2 10.9 %conditional.14 = (bf16[512,1024]{1,0:T(8,128)(2,1)}, bf16[512,4096]{1,0:T(8,128)(2,1)S(1)}) conditional(s32[]{:T(128)} %convert_element_type.174, (bf16[512,1024]{1,0:T(8,128)(2,1)}, bf16[4096,1024]{1,0:T(8,128)(2,1)}) %tuple.87, (bf16[512,4096]{1,0:T(8,128)(2,1)}, bf16[4096,1024]{1,0:T(8,128)(2,1)}) %tuple.88), branch_computations={%region_3.0_spmd, %region_4.0_spmd} | conditional | flops 4297064448 | bytes 17825810 | solution.py:87
  218.4 10.1 %convolution_convert_fusion.3 = bf16[512,1024]{1,0:T(8,128)(2,1)} fusion(bf16[512,4096]{1,0:T(8,128)(2,1)} %get-tuple-element.109, bf16[4096,1024]{1,0:T(8,128)(2,1)} %get-tuple-element.110), kind=kOutput, calls=%fused_computation.3 | convolution fusion | flops 4295491584 | bytes 13631488 | tf_op jit(solution)/shard_map/phase_a/cond/branch_1_fun/dot_general | solution.py:78
  232.6 13.1 %conditional.15 = (bf16[512,1024]{1,0:T(8,128)(2,1)}, bf16[512,4096]{1,0:T(8,128)(2,1)}) conditional(s32[]{:T(128)} %convert_element_type.174, (bf16[512,1024]{1,0:T(8,128)(2,1)}, bf16[4096,1024]{1,0:T(8,128)(2,1)}) %tuple.89, (bf16[512,4096]{1,0:T(8,128)(2,1)}, bf16[4096,1024]{1,0:T(8,128)(2,1)}) %tuple.90), branch_computations={%region_5.0_spmd, %region_6.0_spmd} | conditional | flops 4297064448 | bytes 17825810 | solution.py:87
  233.0 10.1 %convolution_convert_fusion.5 = bf16[512,1024]{1,0:T(8,128)(2,1)} fusion(bf16[512,4096]{1,0:T(8,128)(2,1)} %get-tuple-element.113, bf16[4096,1024]{1,0:T(8,128)(2,1)} %get-tuple-element.114), kind=kOutput, calls=%fused_computation.5 | convolution fusion | flops 4295491584 | bytes 13631488 | tf_op jit(solution)/shard_map/phase_a/cond/branch_1_fun/dot_general | solution.py:78
  253.5 13.5 %conditional.16 = (bf16[512,1024]{1,0:T(8,128)(2,1)S(1)}, f32[512,4096]{1,0:T(8,128)}) conditional(s32[]{:T(128)} %convert_element_type.174, (bf16[512,1024]{1,0:T(8,128)(2,1)S(1)}, bf16[4096,1024]{1,0:T(8,128)(2,1)}) %tuple.91, (bf16[512,4096]{1,0:T(8,128)(2,1)}, bf16[4096,1024]{1,0:T(8,128)(2,1)}) %tuple.92), branch_computations={%region_7.0_spmd, %region_8.0_spmd} | conditional | flops 4299161600 | bytes 22020116 | solution.py:87
  253.5 9.1 %convolution_convert_fusion.7 = bf16[512,1024]{1,0:T(8,128)(2,1)S(1)} fusion(bf16[512,4096]{1,0:T(8,128)(2,1)} %get-tuple-element.117, bf16[4096,1024]{1,0:T(8,128)(2,1)} %get-tuple-element.118), kind=kOutput, calls=%fused_computation.8 | convolution fusion | flops 4295491584 | bytes 13631488 | tf_op jit(solution)/shard_map/phase_a/cond/branch_1_fun/dot_general | solution.py:78
  276.3 9.8 %abs_reduce_fusion.1 = (f32[8,4096]{1,0:T(8,128)S(1)}, f32[8,64,4096]{2,1,0:T(8,128)}) fusion(f32[8,4096]{1,0:T(8,128)S(1)} %broadcast_bitcast_fusion.4, s32[1,2,8,64,4096]{4,3,2,1,0:T(8,128)} %param.25, bf16[8,64,4096]{2,1,0:T(8,128)(2,1)S(1)} %copy-done.2, f32[8,4096]{1,0:T(8,128)S(1)} %broadcast_bitcast_fusion.5, ...), kind=kLoop, calls=%fused_computation.99 | loop fusion | flops 23035904 | bytes 33947648 | tf_op jit(solution)/shard_map/phase_a/reduce_max | solution.py:130
  286.3 16.9 %pmax.14 = f32[8,32]{0,1:T(8,128)S(1)} all-reduce(f32[8,32]{0,1:T(8,128)S(1)} %bitcast_reduce_fusion.1), channel_id=1, replica_groups=mesh['dp'=4,'section'=2,'tensor'=4] {'tensor'}, use_global_device_ids=true, to_apply=%region_11.0 | all-reduce | flops 256 | bytes 2048 | tf_op jit(solution)/shard_map/phase_a/pmax | solution.py:131
  303.3 9.0 %multiply_convert_fusion.1 = bf16[8,64,4096]{2,1,0:T(8,128)(2,1)S(1)} fusion(f32[8,64,4096]{2,1,0:T(8,128)} %get-tuple-element.191, f32[8,4096]{1,0:T(8,128)S(1)} %get-tuple-element.210, f32[8,4096]{1,0:T(8,128)S(1)} %get-tuple-element.211), kind=kLoop, calls=%fused_computation.89 | loop fusion | flops 56623104 | bytes 12845056 | tf_op jit(solution)/shard_map/phase_a/convert_element_type | solution.py:136
  315.6 10.5 %add_convert_fusion.1 = bf16[512,4096]{1,0:T(8,128)(2,1)} fusion(f32[512,4096]{1,0:T(8,128)} %get-tuple-element.177, bf16[512,4096]{1,0:T(8,128)(2,1)} %collective-permute-done.12, bf16[512,4096]{1,0:T(8,128)(2,1)} %collective-permute-done.11, bf16[512,4096]{1,0:T(8,128)(2,1)} %collective-permute-done.10), kind=kLoop, calls=%fused_computation.86 | loop fusion | flops 14680064 | bytes 25165824 | tf_op jit(solution)/shard_map/phase_a/convert_element_type | solution.py:140
  354.8 32.4 %collective-permute-done.13 = bf16[8,64,4096]{2,1,0:T(8,128)(2,1)S(1)} collective-permute-done((bf16[8,64,4096]{2,1,0:T(8,128)(2,1)S(1)}, bf16[8,64,4096]{2,1,0:T(8,128)(2,1)S(1)}, u32[]{:S(2)}, u32[]{:S(2)}) %collective-permute-start.13) | collective-permute-done | bytes 4194336 | tf_op jit(solution)/shard_map/phase_a/ppermute | solution.py:164
  399.0 18.8 %collective-permute-done.14 = bf16[512,1024]{1,0:T(8,128)(2,1)} collective-permute-done((bf16[512,1024]{1,0:T(8,128)(2,1)S(1)}, bf16[512,1024]{1,0:T(8,128)(2,1)}, u32[]{:S(2)}, u32[]{:S(2)}) %collective-permute-start.14) | collective-permute-done | bytes 1048608 | tf_op jit(solution)/shard_map/phase_a/ppermute | solution.py:59
  423.3 17.6 %collective-permute-done.20 = bf16[512,1024]{1,0:T(8,128)(2,1)} collective-permute-done((bf16[512,1024]{1,0:T(8,128)(2,1)S(1)}, bf16[512,1024]{1,0:T(8,128)(2,1)}, u32[]{:S(2)}, u32[]{:S(2)}) %collective-permute-start.20) | collective-permute-done | bytes 1048608 | tf_op jit(solution)/shard_map/phase_a/ppermute | solution.py:59
  440.9 24.0 %conditional.21 = (bf16[4096,1024]{1,0:T(8,128)(2,1)}) conditional(s32[]{:T(128)} %convert_element_type.174, (bf16[512,4096]{1,0:T(8,128)(2,1)}, bf16[512,4096]{1,0:T(8,128)(2,1)}, bf16[512,4096]{1,0:T(8,128)(2,1)}, bf16[512,4096]{1,0:T(8,128)(2,1)}, bf16[512,1024]{1,0:T(8,128)(2,1)S(1)}, /*index=5*/bf16[512,1024]{1,0:T(8,128)(2,1)}, ...), branch_computations={%region_26.27_spmd, %region_27.28_spmd} | conditional | flops 17263755264 | bytes 29360136
  441.1 23.8 %fusion.18 = bf16[4096,1024]{1,0:T(8,128)(2,1)} fusion(bf16[512,4096]{1,0:T(8,128)(2,1)} %get-tuple-element.146, bf16[512,4096]{1,0:T(8,128)(2,1)} %get-tuple-element.145, bf16[512,4096]{1,0:T(8,128)(2,1)} %get-tuple-element.144, bf16[512,4096]{1,0:T(8,128)(2,1)} %get-tuple-element.143, bf16[512,1024]{1,0:T(8,128)(2,1)} %get-tuple-element.150, ...), kind=kOutput, calls=%fused_computation.34 | convolution fusion | flops 17263755264 | bytes 29360128 | tf_op jit(solution)/shard_map/weight_grad/cond/branch_1_fun/dot_general | solution.py:171
  465.0 10.8 %conditional.17 = (bf16[512,1024]{1,0:T(8,128)(2,1)S(1)}, bf16[512,4096]{1,0:T(8,128)(2,1)}) conditional(s32[]{:T(128)} %convert_element_type.182, (bf16[512,1024]{1,0:T(8,128)(2,1)}, bf16[4096,1024]{1,0:T(8,128)(2,1)}) %tuple.93, (bf16[512,4096]{1,0:T(8,128)(2,1)}, bf16[4096,1024]{1,0:T(8,128)(2,1)}) %tuple.94), branch_computations={%region_14.15_spmd, %region_15.16_spmd} | conditional | flops 4297064448 | bytes 17825810 | solution.py:87
  465.4 10.2 %convolution_convert_fusion.8 = bf16[512,4096]{1,0:T(8,128)(2,1)} fusion(bf16[512,1024]{1,0:T(8,128)(2,1)} %get-tuple-element.119, bf16[4096,1024]{1,0:T(8,128)(2,1)} %get-tuple-element.120), kind=kOutput, calls=%fused_computation.9 | convolution fusion | flops 4297064448 | bytes 13631488 | tf_op jit(solution)/shard_map/phase_b/cond/branch_0_fun/dot_general | solution.py:82
  479.2 10.6 %conditional.18 = (bf16[512,1024]{1,0:T(8,128)(2,1)S(1)}, bf16[512,4096]{1,0:T(8,128)(2,1)}) conditional(s32[]{:T(128)} %convert_element_type.182, (bf16[512,1024]{1,0:T(8,128)(2,1)}, bf16[4096,1024]{1,0:T(8,128)(2,1)}) %tuple.95, (bf16[512,4096]{1,0:T(8,128)(2,1)}, bf16[4096,1024]{1,0:T(8,128)(2,1)}) %tuple.96), branch_computations={%region_16.17_spmd, %region_17.18_spmd} | conditional | flops 4297064448 | bytes 17825810 | solution.py:87
  479.2 10.3 %convolution_convert_fusion.10 = bf16[512,4096]{1,0:T(8,128)(2,1)} fusion(bf16[512,1024]{1,0:T(8,128)(2,1)} %get-tuple-element.123, bf16[4096,1024]{1,0:T(8,128)(2,1)} %get-tuple-element.124), kind=kOutput, calls=%fused_computation.11 | convolution fusion | flops 4297064448 | bytes 13631488 | tf_op jit(solution)/shard_map/phase_b/cond/branch_0_fun/dot_general | solution.py:82
  492.2 11.4 %conditional.19 = (bf16[512,1024]{1,0:T(8,128)(2,1)}, bf16[512,4096]{1,0:T(8,128)(2,1)}) conditional(s32[]{:T(128)} %convert_element_type.182, (bf16[512,1024]{1,0:T(8,128)(2,1)}, bf16[4096,1024]{1,0:T(8,128)(2,1)}) %tuple.97, (bf16[512,4096]{1,0:T(8,128)(2,1)}, bf16[4096,1024]{1,0:T(8,128)(2,1)}) %tuple.98), branch_computations={%region_18.19_spmd, %region_19.20_spmd} | conditional | flops 4297064448 | bytes 17825810 | solution.py:87
  492.2 10.3 %convolution_convert_fusion.12 = bf16[512,4096]{1,0:T(8,128)(2,1)} fusion(bf16[512,1024]{1,0:T(8,128)(2,1)} %get-tuple-element.127, bf16[4096,1024]{1,0:T(8,128)(2,1)} %get-tuple-element.128), kind=kOutput, calls=%fused_computation.13 | convolution fusion | flops 4297064448 | bytes 13631488 | tf_op jit(solution)/shard_map/phase_b/cond/branch_0_fun/dot_general | solution.py:82
  509.5 10.4 %conditional.20 = (bf16[512,1024]{1,0:T(8,128)(2,1)S(1)}, f32[512,4096]{1,0:T(8,128)}) conditional(s32[]{:T(128)} %convert_element_type.182, (bf16[512,1024]{1,0:T(8,128)(2,1)S(1)}, bf16[4096,1024]{1,0:T(8,128)(2,1)}) %tuple.99, (bf16[512,4096]{1,0:T(8,128)(2,1)}, bf16[4096,1024]{1,0:T(8,128)(2,1)}) %tuple.100), branch_computations={%region_20.21_spmd, %region_21.22_spmd} | conditional | flops 4299161600 | bytes 22020116 | solution.py:87
  509.7 10.1 %fusion.1 = f32[512,4096]{1,0:T(8,128)} fusion(bf16[512,1024]{1,0:T(8,128)(2,1)S(1)} %get-tuple-element.131, bf16[4096,1024]{1,0:T(8,128)(2,1)} %get-tuple-element.132), kind=kOutput, calls=%fused_computation.16 | convolution fusion | flops 4299161600 | bytes 17825792 | tf_op jit(solution)/shard_map/phase_b/cond/branch_0_fun/dot_general | solution.py:82
  522.3 20.6 %collective-permute-done.23 = bf16[512,4096]{1,0:T(8,128)(2,1)} collective-permute-done((bf16[512,4096]{1,0:T(8,128)(2,1)}, bf16[512,4096]{1,0:T(8,128)(2,1)}, u32[]{:S(2)}, u32[]{:S(2)}) %collective-permute-start.23) | collective-permute-done | bytes 4194336 | tf_op jit(solution)/shard_map/phase_b/ppermute | solution.py:66
  542.9 55.0 %collective-permute-done.24 = bf16[512,4096]{1,0:T(8,128)(2,1)} collective-permute-done((bf16[512,4096]{1,0:T(8,128)(2,1)}, bf16[512,4096]{1,0:T(8,128)(2,1)}, u32[]{:S(2)}, u32[]{:S(2)}) %collective-permute-start.24) | collective-permute-done | bytes 4194336 | tf_op jit(solution)/shard_map/phase_b/ppermute | solution.py:66
  597.9 8.7 %add_convert_fusion = bf16[512,4096]{1,0:T(8,128)(2,1)S(1)} fusion(f32[512,4096]{1,0:T(8,128)} %get-tuple-element.185, bf16[512,4096]{1,0:T(8,128)(2,1)} %collective-permute-done.25, bf16[512,4096]{1,0:T(8,128)(2,1)} %collective-permute-done.24, bf16[512,4096]{1,0:T(8,128)(2,1)} %collective-permute-done.23), kind=kLoop, calls=%fused_computation.74 | loop fusion | flops 14680064 | bytes 25165824 | tf_op jit(solution)/shard_map/phase_b/convert_element_type | solution.py:140
  613.8 19.1 %pmax.15 = f32[8,32]{0,1:T(8,128)S(1)} all-reduce(f32[8,32]{0,1:T(8,128)S(1)} %bitcast_reduce_fusion), channel_id=1, replica_groups=mesh['dp'=4,'section'=2,'tensor'=4] {'tensor'}, use_global_device_ids=true, to_apply=%region_24.25 | all-reduce | flops 256 | bytes 2048 | tf_op jit(solution)/shard_map/phase_b/pmax | solution.py:131
  633.2 24.0 %fusion.58 = (bf16[1,8,64,4096]{3,2,1,0:T(8,128)(2,1)}, bf16[1,8,64,4096]{3,2,1,0:T(8,128)(2,1)}) fusion(bf16[8,64,4096]{2,1,0:T(8,128)(2,1)} %copy-done.6, f32[8,64,4096]{2,1,0:T(8,128)} %copy-done, bf16[8,64,4096]{2,1,0:T(8,128)(2,1)} %copy-done.8, f32[8,64]{1,0:T(8,128)S(1)} %broadcast_multiply_fusion, f32[8,64]{1,0:T(8,128)S(1)} %copy-done.18, ...), kind=kLoop, calls=%fused_computation.106 | loop fusion | flops 144703488 | bytes 50991104 | tf_op jit(solution)/shard_map/broadcast_in_dim | solution.py:197
  657.2 25.6 %reduce-scatter.2.cloned.1.call-done = bf16[1024,1024]{1,0:T(8,128)(2,1)} async-done(((bf16[4096,1024]{1,0:T(8,128)(2,1)}), bf16[1024,1024]{1,0:T(8,128)(2,1)}) %reduce-scatter.2.cloned.1.call-update) | async-done | bytes 2097168 | tf_op jit(solution)/shard_map/weight_grad/reduce_scatter | solution.py:184
  (155 shorter events, 150.7 us)
Async XLA Ops:
  13.3 190.6 %all-to-all-start = ((bf16[4,1024,1024]{2,1,0:T(8,128)(2,1)}), bf16[4,1024,1024]{2,1,0:T(8,128)(2,1)}, u32[]{:S(2)}, u32[]{:S(2)}) async-start(bf16[4,1024,1024]{2,1,0:T(8,128)(2,1)} %stack.10), calls=%async_computation | async-start | bytes 16777216 | tf_op jit(solution)/shard_map/all_to_all | solution.py:73
  19.8 663.0 %reduce-scatter.2.cloned.1.call-start = ((), (), s32[]{:S(2)}) async-start(), calls=%async_computation.2 | async-start | bytes 10485760 | tf_op jit(solution)/shard_map/weight_grad/reduce_scatter | solution.py:184
  31.5 172.5 %collective-permute-start.1 = (bf16[512,4096]{1,0:T(8,128)(2,1)}, bf16[512,4096]{1,0:T(8,128)(2,1)}, u32[]{:S(2)}, u32[]{:S(2)}) collective-permute-start(bf16[512,4096]{1,0:T(8,128)(2,1)} %bitcast.6), channel_id=1, source_target_pairs={{0,8},{8,0},{16,24},{24,16},{1,9},{9,1},{17,25},{25,17},{2,10},{10... | collective-permute-start | bytes 12582920 | tf_op jit(solution)/shard_map/phase_a/ppermute | solution.py:59
  35.7 182.5 %collective-permute-start.4 = (bf16[512,4096]{1,0:T(8,128)(2,1)}, bf16[512,4096]{1,0:T(8,128)(2,1)}, u32[]{:S(2)}, u32[]{:S(2)}) collective-permute-start(bf16[512,4096]{1,0:T(8,128)(2,1)} %bitcast.6), channel_id=1, source_target_pairs={{0,16},{8,24},{16,0},{24,8},{1,17},{9,25},{17,1},{25,9},{2,18},{10... | collective-permute-start | bytes 12582920 | tf_op jit(solution)/shard_map/phase_a/ppermute | solution.py:59
  39.1 193.5 %collective-permute-start.7 = (bf16[512,4096]{1,0:T(8,128)(2,1)}, bf16[512,4096]{1,0:T(8,128)(2,1)}, u32[]{:S(2)}, u32[]{:S(2)}) collective-permute-start(bf16[512,4096]{1,0:T(8,128)(2,1)} %bitcast.6), channel_id=1, source_target_pairs={{0,24},{8,16},{16,8},{24,0},{1,25},{9,17},{17,9},{25,1},{2,26},{10... | collective-permute-start | bytes 12582920 | tf_op jit(solution)/shard_map/phase_a/ppermute | solution.py:59
  44.9 2.4 collective-permute-start
  45.6 172.6 %collective-permute-start.3 = (bf16[512,1024]{1,0:T(8,128)(2,1)}, bf16[512,1024]{1,0:T(8,128)(2,1)}, u32[]{:S(2)}, u32[]{:S(2)}) collective-permute-start(bf16[512,1024]{1,0:T(8,128)(2,1)} %get-tuple-element.202), channel_id=1, source_target_pairs={{4,20},{12,28},{20,4},{28,12},{5,21},{13,29},{21,5},{29,13},{6,22}... | collective-permute-start | bytes 3145736 | tf_op jit(solution)/shard_map/phase_a/ppermute | solution.py:59
  48.3 184.3 %collective-permute-start.6 = (bf16[512,1024]{1,0:T(8,128)(2,1)S(1)}, bf16[512,1024]{1,0:T(8,128)(2,1)}, u32[]{:S(2)}, u32[]{:S(2)}) collective-permute-start(bf16[512,1024]{1,0:T(8,128)(2,1)S(1)} %get-tuple-element.201), channel_id=1, source_target_pairs={{4,28},{12,20},{20,12},{28,4},{5,29},{13,21},{21,13},{29,5},{6,30}... | collective-permute-start | bytes 3145736 | tf_op jit(solution)/shard_map/phase_a/ppermute | solution.py:59
  214.7 52.3 %collective-permute-start.2 = (bf16[512,1024]{1,0:T(8,128)(2,1)}, bf16[512,1024]{1,0:T(8,128)(2,1)}, u32[]{:S(2)}, u32[]{:S(2)}) collective-permute-start(bf16[512,1024]{1,0:T(8,128)(2,1)} %get-tuple-element.170), channel_id=1, source_target_pairs={{0,8},{8,0},{16,24},{24,16},{1,9},{9,1},{17,25},{25,17},{2,10},{10... | collective-permute-start | bytes 3145736 | tf_op jit(solution)/shard_map/phase_a/ppermute | solution.py:66
  229.1 42.8 %collective-permute-start.5 = (bf16[512,1024]{1,0:T(8,128)(2,1)}, bf16[512,1024]{1,0:T(8,128)(2,1)}, u32[]{:S(2)}, u32[]{:S(2)}) collective-permute-start(bf16[512,1024]{1,0:T(8,128)(2,1)} %get-tuple-element.171), channel_id=1, source_target_pairs={{0,16},{8,24},{16,0},{24,8},{1,17},{9,25},{17,1},{25,9},{2,18},{10... | collective-permute-start | bytes 3145736 | tf_op jit(solution)/shard_map/phase_a/ppermute | solution.py:66
  245.7 29.2 %collective-permute-start.8 = (bf16[512,1024]{1,0:T(8,128)(2,1)}, bf16[512,1024]{1,0:T(8,128)(2,1)}, u32[]{:S(2)}, u32[]{:S(2)}) collective-permute-start(bf16[512,1024]{1,0:T(8,128)(2,1)} %get-tuple-element.172), channel_id=1, source_target_pairs={{0,24},{8,16},{16,8},{24,0},{1,25},{9,17},{17,9},{25,1},{2,26},{10... | collective-permute-start | bytes 3145736 | tf_op jit(solution)/shard_map/phase_a/ppermute | solution.py:66
  248.2 28.2 %copy-start.9 = (f32[8,4096]{1,0:T(8,128)}, f32[8,4096]{1,0:T(8,128)S(1)}, u32[]{:S(2)}) copy-start(f32[8,4096]{1,0:T(8,128)S(1)} %broadcast_bitcast_fusion.4) | copy-start | bytes 393220
  248.2 67.4 %collective-permute-start.11 = (bf16[512,4096]{1,0:T(8,128)(2,1)}, bf16[512,4096]{1,0:T(8,128)(2,1)}, u32[]{:S(2)}, u32[]{:S(2)}) collective-permute-start(bf16[512,4096]{1,0:T(8,128)(2,1)} %copy-done.21), channel_id=1, source_target_pairs={{4,20},{12,28},{20,4},{28,12},{5,21},{13,29},{21,5},{29,13},{6,22}... | collective-permute-start | bytes 12582920 | tf_op jit(solution)/shard_map/phase_a/ppermute | solution.py:66
  250.8 64.8 %collective-permute-start.12 = (bf16[512,4096]{1,0:T(8,128)(2,1)}, bf16[512,4096]{1,0:T(8,128)(2,1)}, u32[]{:S(2)}, u32[]{:S(2)}) collective-permute-start(bf16[512,4096]{1,0:T(8,128)(2,1)} %get-tuple-element.176), channel_id=1, source_target_pairs={{4,28},{12,20},{20,12},{28,4},{5,29},{13,21},{21,13},{29,5},{6,30}... | collective-permute-start | bytes 12582920 | tf_op jit(solution)/shard_map/phase_a/ppermute | solution.py:66
  267.0 48.6 %collective-permute-start.10 = (bf16[512,4096]{1,0:T(8,128)(2,1)}, bf16[512,4096]{1,0:T(8,128)(2,1)}, u32[]{:S(2)}, u32[]{:S(2)}) collective-permute-start(bf16[512,4096]{1,0:T(8,128)(2,1)} %copy-done.20), channel_id=1, source_target_pairs={{4,12},{12,4},{20,28},{28,20},{5,13},{13,5},{21,29},{29,21},{6,14}... | collective-permute-start | bytes 12582920 | tf_op jit(solution)/shard_map/phase_a/ppermute | solution.py:66
  312.3 13.8 %collective-permute-start.9 = (bf16[8,64,4096]{2,1,0:T(8,128)(2,1)S(1)}, bf16[8,64,4096]{2,1,0:T(8,128)(2,1)}, u32[]{:S(2)}, u32[]{:S(2)}) collective-permute-start(bf16[8,64,4096]{2,1,0:T(8,128)(2,1)S(1)} %multiply_convert_fusion.1), channel_id=1, source_target_pairs={{0,4},{1,5},{2,6},{3,7},{8,12},{9,13},{10,14},{11,15},{16,20},{17,... | collective-permute-start | bytes 12582920 | tf_op jit(solution)/shard_map/phase_a/ppermute | solution.py:159
  345.5 41.7 %collective-permute-start.13 = (bf16[8,64,4096]{2,1,0:T(8,128)(2,1)S(1)}, bf16[8,64,4096]{2,1,0:T(8,128)(2,1)S(1)}, u32[]{:S(2)}, u32[]{:S(2)}) collective-permute-start(bf16[8,64,4096]{2,1,0:T(8,128)(2,1)S(1)} %fusion.37), channel_id=1, source_target_pairs={{4,0},{5,1},{6,2},{7,3},{12,8},{13,9},{14,10},{15,11},{20,16},{21,... | collective-permute-start | bytes 12582920 | tf_op jit(solution)/shard_map/phase_a/ppermute | solution.py:164
  346.7 49.6 %collective-permute-start.15 = (bf16[512,4096]{1,0:T(8,128)(2,1)}, bf16[512,4096]{1,0:T(8,128)(2,1)}, u32[]{:S(2)}, u32[]{:S(2)}) collective-permute-start(bf16[512,4096]{1,0:T(8,128)(2,1)} %bitcast.17), channel_id=1, source_target_pairs={{4,12},{12,4},{20,28},{28,20},{5,13},{13,5},{21,29},{29,21},{6,14}... | collective-permute-start | bytes 12582920 | tf_op jit(solution)/shard_map/phase_a/ppermute | solution.py:59
  349.5 49.5 %collective-permute-start.18 = (bf16[512,4096]{1,0:T(8,128)(2,1)}, bf16[512,4096]{1,0:T(8,128)(2,1)}, u32[]{:S(2)}, u32[]{:S(2)}) collective-permute-start(bf16[512,4096]{1,0:T(8,128)(2,1)} %bitcast.17), channel_id=1, source_target_pairs={{4,20},{12,28},{20,4},{28,12},{5,21},{13,29},{21,5},{29,13},{6,22}... | collective-permute-start | bytes 12582920 | tf_op jit(solution)/shard_map/phase_a/ppermute | solution.py:59
  352.1 46.9 %collective-permute-start.21 = (bf16[512,4096]{1,0:T(8,128)(2,1)}, bf16[512,4096]{1,0:T(8,128)(2,1)}, u32[]{:S(2)}, u32[]{:S(2)}) collective-permute-start(bf16[512,4096]{1,0:T(8,128)(2,1)} %bitcast.17), channel_id=1, source_target_pairs={{4,28},{12,20},{20,12},{28,4},{5,29},{13,21},{21,13},{29,5},{6,30}... | collective-permute-start | bytes 12582920 | tf_op jit(solution)/shard_map/phase_a/ppermute | solution.py:59
  389.7 28.0 %collective-permute-start.14 = (bf16[512,1024]{1,0:T(8,128)(2,1)S(1)}, bf16[512,1024]{1,0:T(8,128)(2,1)}, u32[]{:S(2)}, u32[]{:S(2)}) collective-permute-start(bf16[512,1024]{1,0:T(8,128)(2,1)S(1)} %get-tuple-element.196), channel_id=1, source_target_pairs={{0,8},{8,0},{16,24},{24,16},{1,9},{9,1},{17,25},{25,17},{2,10},{10... | collective-permute-start | bytes 3145736 | tf_op jit(solution)/shard_map/phase_a/ppermute | solution.py:59
  392.9 30.5 %collective-permute-start.17 = (bf16[512,1024]{1,0:T(8,128)(2,1)S(1)}, bf16[512,1024]{1,0:T(8,128)(2,1)}, u32[]{:S(2)}, u32[]{:S(2)}) collective-permute-start(bf16[512,1024]{1,0:T(8,128)(2,1)S(1)} %get-tuple-element.199), channel_id=1, source_target_pairs={{0,16},{8,24},{16,0},{24,8},{1,17},{9,25},{17,1},{25,9},{2,18},{10... | collective-permute-start | bytes 3145736 | tf_op jit(solution)/shard_map/phase_a/ppermute | solution.py:59
  396.3 44.6 %collective-permute-start.20 = (bf16[512,1024]{1,0:T(8,128)(2,1)S(1)}, bf16[512,1024]{1,0:T(8,128)(2,1)}, u32[]{:S(2)}, u32[]{:S(2)}) collective-permute-start(bf16[512,1024]{1,0:T(8,128)(2,1)S(1)} %get-tuple-element.198), channel_id=1, source_target_pairs={{0,24},{8,16},{16,8},{24,0},{1,25},{9,17},{17,9},{25,1},{2,26},{10... | collective-permute-start | bytes 3145736 | tf_op jit(solution)/shard_map/phase_a/ppermute | solution.py:59
  475.8 67.2 %collective-permute-start.23 = (bf16[512,4096]{1,0:T(8,128)(2,1)}, bf16[512,4096]{1,0:T(8,128)(2,1)}, u32[]{:S(2)}, u32[]{:S(2)}) collective-permute-start(bf16[512,4096]{1,0:T(8,128)(2,1)} %get-tuple-element.182), channel_id=1, source_target_pairs={{0,8},{8,0},{16,24},{24,16},{1,9},{9,1},{17,25},{25,17},{2,10},{10... | collective-permute-start | bytes 12582920 | tf_op jit(solution)/shard_map/phase_b/ppermute | solution.py:66
  489.8 108.1 %collective-permute-start.24 = (bf16[512,4096]{1,0:T(8,128)(2,1)}, bf16[512,4096]{1,0:T(8,128)(2,1)}, u32[]{:S(2)}, u32[]{:S(2)}) collective-permute-start(bf16[512,4096]{1,0:T(8,128)(2,1)} %get-tuple-element.183), channel_id=1, source_target_pairs={{0,16},{8,24},{16,0},{24,8},{1,17},{9,25},{17,1},{25,9},{2,18},{10... | collective-permute-start | bytes 12582920 | tf_op jit(solution)/shard_map/phase_b/ppermute | solution.py:66
  503.7 94.2 %collective-permute-start.25 = (bf16[512,4096]{1,0:T(8,128)(2,1)}, bf16[512,4096]{1,0:T(8,128)(2,1)}, u32[]{:S(2)}, u32[]{:S(2)}) collective-permute-start(bf16[512,4096]{1,0:T(8,128)(2,1)} %get-tuple-element.184), channel_id=1, source_target_pairs={{0,24},{8,16},{16,8},{24,0},{1,25},{9,17},{17,9},{25,1},{2,26},{10... | collective-permute-start | bytes 12582920 | tf_op jit(solution)/shard_map/phase_b/ppermute | solution.py:66
  507.1 1.5 collective-permute-start.16
  507.8 14.0 %collective-permute-start.19 = (bf16[512,1024]{1,0:T(8,128)(2,1)}, bf16[512,1024]{1,0:T(8,128)(2,1)S(1)}, u32[]{:S(2)}, u32[]{:S(2)}) collective-permute-start(bf16[512,1024]{1,0:T(8,128)(2,1)} %copy-done.16), channel_id=1, source_target_pairs={{4,20},{12,28},{20,4},{28,12},{5,21},{13,29},{21,5},{29,13},{6,22}... | collective-permute-start | bytes 3145736 | tf_op jit(solution)/shard_map/phase_b/ppermute | solution.py:66
  508.6 13.4 %collective-permute-start.22 = (bf16[512,1024]{1,0:T(8,128)(2,1)}, bf16[512,1024]{1,0:T(8,128)(2,1)S(1)}, u32[]{:S(2)}, u32[]{:S(2)}) collective-permute-start(bf16[512,1024]{1,0:T(8,128)(2,1)} %get-tuple-element.180), channel_id=1, source_target_pairs={{4,28},{12,20},{20,12},{28,4},{5,29},{13,21},{21,13},{29,5},{6,30}... | collective-permute-start | bytes 3145736 | tf_op jit(solution)/shard_map/phase_b/ppermute | solution.py:66
  522.0 84.6 %slice-start = ((s8[8388608]{0:T(1024)(128)(4,1)}), s8[4194304]{0:T(1024)(128)(4,1)S(1)}, s32[]{:S(2)}) async-start(s8[8388608]{0:T(1024)(128)(4,1)} %bitcast.102), calls=%async_computation.3 | async-start | bytes 8388608
  522.3 84.3 %copy-start.3 = (bf16[512,4096]{1,0:T(8,128)(2,1)}, bf16[512,4096]{1,0:T(8,128)(2,1)S(1)}, u32[]{:S(2)}) copy-start(bf16[512,4096]{1,0:T(8,128)(2,1)S(1)} %constant_dynamic-update-slice_fusion) | copy-start | bytes 12582916
  606.7 26.5 %copy-start.12 = (f32[8,4096]{1,0:T(8,128)S(1)}, f32[8,4096]{1,0:T(8,128)}, u32[]{:S(2)}) copy-start(f32[8,4096]{1,0:T(8,128)} %copy-done.11) | copy-start | bytes 393220
  (25 other events, 241.6 us)
Sparse Core Ops, SparseCore 0:
  465.1 217.6 reduce-scatter.1
